TPU v7x, 256 devices: a whole 4x4x8 slice. The times are simulated.
256 devices in a mesh: row: 128 (over z, y_lo, x, core), ch: 2 (over y_hi).
Axes of the slice: x: 4, y: 4 (y_hi: 2, y_lo: 2; y = y_hi * 2 + y_lo), z: 8, core: 2. Of those that a mesh axis runs over, the one named last changes fastest.
Arguments:
- pair_rep: bfloat16 [384, 384, 128], P('row'), may hold values from -6 to 6
- res_mask: int32 [384], replicated, may hold values 0 or 1
- in_gain: float32 [128], replicated, may hold values from 0.5 to 1.5
- w_left: bfloat16 [128, 128], P(None, 'ch'), may hold values from -0.5 to 0.5
- w_left_gate: bfloat16 [128, 128], P(None, 'ch'), may hold values from -0.5 to 0.5
- w_right: bfloat16 [128, 128], P(None, 'ch'), may hold values from -0.5 to 0.5
- w_right_gate: bfloat16 [128, 128], P(None, 'ch'), may hold values from -0.5 to 0.5
- w_gate: bfloat16 [128, 128], replicated, may hold values from -0.5 to 0.5
- mid_gain: float32 [128], replicated, may hold values from 0.5 to 1.5
- w_out: bfloat16 [128, 128], replicated, may hold values from -0.5 to 0.5
- next_gain: float32 [128], replicated, may hold values from 0.5 to 1.5
Outputs:
- new_pair: bfloat16 [384, 384, 128], P(None, 'row', 'ch')
- new_norm: bfloat16 [384, 384, 128], P(None, 'row', 'ch')
All inputs are finite; a program needn't handle non-finite values.
Results may differ from a plain program's by a relative error of at most 0.0065.
Values may be sent and summed in bfloat16 or wider, within the bound.
A program may use at most 64 MiB of HBM per device.

v0:
```python
import jax
import jax.numpy as jnp
from jax import lax
from jax.sharding import Mesh
from jax.sharding import PartitionSpec as P

ROW = ("row_0", "row_1", "row_2", "row_3")
epsilon = 1e-05


def split_up(array, dim, devices):
    dims = array.shape
    blocks = array.reshape(*dims[:dim], devices, dims[dim] // devices, *dims[dim + 1 :])
    return jnp.moveaxis(blocks, dim, 0)


def in_order(blocks, dim):
    dims = list(blocks.shape[1:])
    dims[dim] *= blocks.shape[0]
    return jnp.moveaxis(blocks, 0, dim).reshape(dims)


def moved_by_axis(blocks, axes, order):
    inside = blocks.shape[1:]
    whole = blocks.reshape(*(lax.axis_size(a) for a in axes), *inside)
    for k in order:
        whole = lax.all_to_all(whole, axes[k], k, k, tiled=True)
    return whole.reshape(-1, *inside)


def exchange_by_chip(array, groups, order, split_dim, concat_dim):
    devices = lax.axis_size(groups[0]) * lax.axis_size(groups[1])
    blocks = split_up(array, split_dim, devices)
    return in_order(moved_by_axis(blocks, groups, order), concat_dim)


def copy_for_each(array, axis):
    copies = jnp.broadcast_to(array, (lax.axis_size(axis), *array.shape))
    return lax.all_to_all(copies, axis, split_axis=0, concat_axis=0, tiled=True)


def over_copies(array, axis):
    return copy_for_each(array, axis).sum(axis=0)


def together(arrays, axis):
    vector, at, gathered = (jnp.concatenate([a.reshape(-1) for a in arrays]), 0, [])
    so_far = over_copies(vector, axis)
    for a in arrays:
        gathered.append(so_far[at : at + a.size].reshape(a.shape))
        at += a.size
    return tuple(gathered)


def sum_at_owner(array, axis, dim):
    blocks = split_up(array, dim, lax.axis_size(axis))
    arrived = lax.all_to_all(blocks, axis, split_axis=0, concat_axis=0, tiled=True)
    return arrived.astype(jnp.float32).sum(axis=0)


def packed_total(arrays, axis):
    vector, at, gathered = (jnp.concatenate([a.reshape(-1) for a in arrays]), 0, [])
    so_far = lax.psum(vector, axis)
    for a in arrays:
        gathered.append(so_far[at : at + a.size].reshape(a.shape))
        at += a.size
    return tuple(gathered)


def normalize(values, scale_gain, along):
    values = values.astype(jnp.float32)
    average = jnp.mean(values, along, keepdims=True)
    centred = values - average
    spread = jnp.mean(centred * centred, along, keepdims=True)
    return centred * lax.rsqrt(spread + epsilon) * scale_gain


def gated(normed, weight, weight_gate, pair_mask):
    values_lin = jnp.einsum("ilc,ch->hil", normed, weight, preferred_element_type=jnp.float32)
    switch = jnp.einsum("ilc,ch->hil", normed, weight_gate, preferred_element_type=jnp.float32)
    return (jax.nn.sigmoid(switch) * values_lin * pair_mask[None]).astype(jnp.bfloat16)


def batched_rows(first, second):
    return lax.dot_general(
        first, second, (((2,), (2,)), ((0,), (0,))), preferred_element_type=jnp.float32
    )


def local(
    pair_rep,
    res_mask,
    in_gain,
    w_left,
    w_left_gate,
    w_right,
    w_right_gate,
    w_gate,
    mid_gain,
    w_out,
    next_gain,
):
    row_count = pair_rep.shape[0]
    channels = pair_rep.shape[2]
    hid_local = w_left.shape[1]
    ch_count = lax.axis_size("ch")
    ch_index = lax.axis_index("ch")
    row_index = lax.axis_index(ROW)
    ch_width = channels // ch_count
    res_float = res_mask.astype(jnp.float32)
    own_mask = lax.dynamic_slice_in_dim(res_float, row_index * row_count, row_count)
    pair_mask = own_mask[:, None] * res_float[None, :]
    normed = normalize(pair_rep, in_gain, 2).astype(jnp.bfloat16)
    left_side = gated(normed, w_left, w_left_gate, pair_mask)
    right_side = gated(normed, w_right, w_right_gate, pair_mask)
    pair_here = exchange_by_chip(pair_rep, (("row_0", "row_1", "row_2"), "row_3"), (1, 0), 1, 0)
    normed_here = normalize(pair_here, in_gain, 2).astype(jnp.bfloat16)
    triangle = batched_rows(right_side, lax.all_gather(left_side, ROW, axis=1, tiled=True))
    einsum_form = "kba,kc->abc"
    hidden_total = hid_local * ch_count
    stat_sums = together((jnp.sum(triangle, 0), jnp.sum(triangle * triangle, 0)), "ch")
    mean_vals = stat_sums[0] / hidden_total
    var_vals = stat_sums[1] / hidden_total - mean_vals * mean_vals
    own_gain = lax.dynamic_slice_in_dim(mid_gain, ch_index * hid_local, hid_local)
    tri_normed = (
        (triangle - mean_vals) * lax.rsqrt(var_vals + epsilon) * own_gain[:, None, None]
    ).astype(jnp.bfloat16)
    w_rows = lax.dynamic_slice_in_dim(w_out, ch_index * hid_local, hid_local, 0)
    partial_terms = jnp.einsum(einsum_form, tri_normed, w_rows, preferred_element_type=jnp.float32)
    update = sum_at_owner(partial_terms.astype(jnp.bfloat16), "ch", 2)
    w_cols = lax.dynamic_slice_in_dim(w_gate, ch_index * ch_width, ch_width, 1)
    gate_vals = jax.nn.sigmoid(
        jnp.einsum("abc,cd->abd", normed_here, w_cols, preferred_element_type=jnp.float32)
    )
    pair_half = lax.dynamic_slice_in_dim(pair_here, ch_index * ch_width, ch_width, 2)
    new_half = (pair_half.astype(jnp.float32) + gate_vals * update).astype(jnp.bfloat16)
    values = new_half.astype(jnp.float32)
    next_sums = packed_total((jnp.sum(values, 2), jnp.sum(values * values, 2)), "ch")
    next_mean = next_sums[0] / channels
    next_var = next_sums[1] / channels - next_mean * next_mean
    own_next = lax.dynamic_slice_in_dim(next_gain, ch_index * ch_width, ch_width)
    norm_half = (
        (values - next_mean[..., None]) * lax.rsqrt(next_var + epsilon)[..., None] * own_next
    ).astype(jnp.bfloat16)
    return (new_half, norm_half)


def solution(mesh):
    split = Mesh(
        mesh.devices.reshape(8, 2, 4, 2, mesh.shape["ch"]),
        ("row_0", "row_1", "row_2", "row_3", "ch"),
    )
    return jax.shard_map(
        local,
        mesh=split,
        in_specs=(
            P(ROW, None, None),
            P(),
            P(),
            P(None, "ch"),
            P(None, "ch"),
            P(None, "ch"),
            P(None, "ch"),
            P(),
            P(),
            P(),
            P(),
        ),
        out_specs=(P(None, ROW, "ch"), P(None, ROW, "ch")),
        check_vma=False,
    )
```

profile of v0, /device:TPU:16, one launch (start us, length us, event | category | flops | bytes accessed | tf_op | source)
XLA Modules:
  0.0 321.3 jit_solution(7978292074478839061)
XLA Ops:
  8.1 1.1 convert_reduce_fusion
  9.2 1.4 fusion.22
  10.6 1.5 fusion.6
  12.2 2.2 fusion.18
  14.4 1.3 reshape.148
  15.8 4.0 %all_to_all.21 = bf16[64,2,3,3,128]{4,0,3,2,1:T(8,128)(2,1)S(1)} all-to-all(bf16[64,2,3,3,128]{4,0,3,2,1:T(8,128)(2,1)S(1)} %copy.83), channel_id=1, replica_groups=mesh['row_0'=8,'row_1'=2,'row_2'=4,'row_3'=2,'ch'=2] {'row_3'}, dimensions={1} | all-to-all | bytes 589824 | tf_op jit(solution)/shard_map/all_to_all | solution.py:27
  19.7 1.0 copy.84
  20.7 12.7 %all-to-all-start.1 = ((bf16[64,2,3,3,128]{4,1,3,2,0:T(2,128)(2,1)}), bf16[64,2,3,3,128]{4,1,3,2,0:T(2,128)(2,1)S(1)}, u32[]{:S(2)}, u32[]{:S(2)}) async-start(bf16[64,2,3,3,128]{4,1,3,2,0:T(2,128)(2,1)} %copy.84), calls=%async_computation.1 | async-start | bytes 589824 | tf_op jit(solution)/shard_map/all_to_all | solution.py:27
  33.4 0.7 dynamic_slice.22
  34.9 1.5 fusion.9
  36.4 1.5 fusion.19
  37.9 10.0 %all-to-all-done.1 = bf16[64,2,3,3,128]{4,1,3,2,0:T(2,128)(2,1)S(1)} async-done(((bf16[64,2,3,3,128]{4,1,3,2,0:T(2,128)(2,1)}), bf16[64,2,3,3,128]{4,1,3,2,0:T(2,128)(2,1)S(1)}, u32[]{:S(2)}, u32[]{:S(2)}) %all-to-all-start.1) | async-done | bytes 294944 | tf_op jit(solution)/shard_map/all_to_all | solution.py:27
  48.4 0.9 convert_reduce_fusion.1
  49.3 1.7 fusion.26
  51.1 200.2 %all-gather.2.cloned.1.call-done = bf16[64,384,384]{2,0,1:T(8,128)(2,1)} async-done(((bf16[64,3,384]{2,0,1:T(8,128)(2,1)}), bf16[64,384,384]{2,0,1:T(8,128)(2,1)}) %all-gather.2.cloned.1.call-update) | async-done | bytes 18874384 | tf_op jit(solution)/shard_map/all_gather | solution.py:118
  251.3 29.4 %fusion.50 = (f32[3,384]{1,0:T(4,128)S(1)}, f32[3,384]{1,0:T(4,128)S(1)}, f32[64,3,384]{2,1,0:T(4,128)S(1)}) fusion(bf16[64,384,384]{2,0,1:T(8,128)(2,1)} %all-gather.2.cloned.1.call-done, bf16[64,3,384]{2,0,1:T(8,128)(2,1)S(1)} %fusion.19), kind=kOutput, calls=%fused_computation.78 | convolution fusion | flops 56841984 | bytes 19325952 | tf_op jit(solution)/shard_map/dot_general | solution.py:85
  281.6 5.0 %all-to-all-start.2 = ((f32[2,1,2304]{2,1,0:T(1,128)}), f32[2,1,2304]{2,1,0:T(1,128)S(1)}, u32[]{:S(2)}, u32[]{:S(2)}) async-start(f32[2,1,2304]{2,1,0:T(1,128)} %broadcast_in_dim.2), calls=%async_computation.2 | async-start | bytes 36864 | tf_op jit(solution)/shard_map/all_to_all | solution.py:39
  286.8 1.3 copy.88
  289.0 0.7 copy.124
  289.7 7.0 %all-to-all-start.3 = ((bf16[2,384,3,64]{1,3,2,0:T(8,128)(2,1)}), bf16[2,384,3,64]{1,3,2,0:T(8,128)(2,1)S(1)}, u32[]{:S(2)}, u32[]{:S(2)}) async-start(bf16[2,384,3,64]{1,3,2,0:T(8,128)(2,1)} %bitcast.39), calls=%async_computation.3 | async-start | bytes 589824 | tf_op jit(solution)/shard_map/all_to_all | solution.py:57
  296.8 1.3 copy.91
  298.6 1.4 all-to-all-done.3
  301.4 11.6 %psum.7 = f32[2304]{0:T(1024)S(1)} all-reduce(f32[2304]{0:T(1024)S(1)} %pad_maximum_fusion.1), channel_id=1, replica_groups=mesh['row_0'=8,'row_1'=2,'row_2'=4,'row_3'=2,'ch'=2] {'ch'}, use_global_device_ids=true, to_apply=%region_10.0 | all-reduce | flops 2304 | bytes 18432 | tf_op jit(solution)/shard_map/psum | solution.py:63
  313.7 0.8 fusion.30
  (50 shorter events, 6.8 us)
Async XLA Ops:
  7.2 281.5 %copy-start = (bf16[128,128]{1,0:T(8,128)(2,1)S(1)}, bf16[128,128]{1,0:T(8,128)(2,1)}, u32[]{:S(2)}) copy-start(bf16[128,128]{1,0:T(8,128)(2,1)} %param.20) | copy-start | bytes 98308
  7.2 244.2 %all-gather.2.cloned.1.call-start = ((), (), s32[]{:S(2)}) async-start(), calls=%async_computation.4 | async-start | bytes 19021824 | tf_op jit(solution)/shard_map/all_gather | solution.py:118
  12.1 287.9 %copy-start.2 = (bf16[128,128]{1,0:T(8,128)(2,1)S(1)}, bf16[128,128]{1,0:T(8,128)(2,1)}, u32[]{:S(2)}) copy-start(bf16[128,128]{1,0:T(8,128)(2,1)} %param.18) | copy-start | bytes 98308
  12.1 287.9 %copy-start.3 = (f32[128]{0:T(128)S(1)}, f32[128]{0:T(128)}, u32[]{:S(2)}) copy-start(f32[128]{0:T(128)} %param.13) | copy-start | bytes 1540
  20.7 27.2 %all-to-all-start.1 = ((bf16[64,2,3,3,128]{4,1,3,2,0:T(2,128)(2,1)}), bf16[64,2,3,3,128]{4,1,3,2,0:T(2,128)(2,1)S(1)}, u32[]{:S(2)}, u32[]{:S(2)}) async-start(bf16[64,2,3,3,128]{4,1,3,2,0:T(2,128)(2,1)} %copy.84), calls=%async_computation.1 | async-start | bytes 589824 | tf_op jit(solution)/shard_map/all_to_all | solution.py:27
  281.6 6.8 %all-to-all-start.2 = ((f32[2,1,2304]{2,1,0:T(1,128)}), f32[2,1,2304]{2,1,0:T(1,128)S(1)}, u32[]{:S(2)}, u32[]{:S(2)}) async-start(f32[2,1,2304]{2,1,0:T(1,128)} %broadcast_in_dim.2), calls=%async_computation.2 | async-start | bytes 36864 | tf_op jit(solution)/shard_map/all_to_all | solution.py:39
  289.7 10.3 %all-to-all-start.3 = ((bf16[2,384,3,64]{1,3,2,0:T(8,128)(2,1)}), bf16[2,384,3,64]{1,3,2,0:T(8,128)(2,1)S(1)}, u32[]{:S(2)}, u32[]{:S(2)}) async-start(bf16[2,384,3,64]{1,3,2,0:T(8,128)(2,1)} %bitcast.39), calls=%async_computation.3 | async-start | bytes 589824 | tf_op jit(solution)/shard_map/all_to_all | solution.py:57
  300.7 13.8 %copy-start.1 = (bf16[384,3,64]{0,2,1:T(8,128)(2,1)}, bf16[384,3,64]{0,2,1:T(8,128)(2,1)S(1)}, u32[]{:S(2)}) copy-start(bf16[384,3,64]{0,2,1:T(8,128)(2,1)S(1)} %get-tuple-element.11) | copy-start | bytes 442372
Sparse Core Ops, SparseCore 0:
  14.5 236.8 all-gather.1
where the time goes:
time: 322 us; the launch traced here: 321 us
  waiting for transfers between devices  212 us (66%)
  matrix products  37 us (11%)
  starting transfers between devices  24.6 us (8%)
  blocking collectives  15.6 us (5%)
  between operations  14.3 us (4%)
  local copies, waits for them, and re-layouts  10.5 us (3%)
  other arithmetic  7.41 us (2%)
    all_gather x1, waiting for transfers between devices, local(): lax.all_gather(left_side, ROW, axis=1, tiled=True)  200 us
    dot_general x1, matrix products, batched_rows(): lax.dot_general(first, second, (((2,), (2,)), ((0,), (0,))), preferred_el...  29.4 us
    all_to_all x1, starting transfers between devices, moved_by_axis(): whole = lax.all_to_all(whole, axes[k], k, k, tiled=True)  12.7 us
    psum x1, blocking collectives, packed_total(): so_far = lax.psum(vector, axis)  11.6 us
    all_to_all x1, waiting for transfers between devices, moved_by_axis(): whole = lax.all_to_all(whole, axes[k], k, k, tiled=True)  10 us
    all_to_all x1, starting transfers between devices, sum_at_owner(): lax.all_to_all(blocks, axis, split_axis=0, concat_axis=0, tiled=True)  6.96 us
  transfers between devices with their start and end apart: 4, of which 4 were waited for; matrix products, arithmetic and copies ran while one was open for 4% of the time, Pallas kernels for 0%

commit v1 on v0

--- a/solution.py
+++ b/solution.py
@@ -115,7 +115,12 @@
     right_side = gated(normed, w_right, w_right_gate, pair_mask)
     pair_here = exchange_by_chip(pair_rep, (("row_0", "row_1", "row_2"), "row_3"), (1, 0), 1, 0)
     normed_here = normalize(pair_here, in_gain, 2).astype(jnp.bfloat16)
-    triangle = batched_rows(right_side, lax.all_gather(left_side, ROW, axis=1, tiled=True))
+    triangle = batched_rows(
+        right_side,
+        jnp.concatenate(
+            lax.all_to_all(jnp.stack([left_side] * lax.axis_size(ROW)), ROW, 0, 0), axis=1
+        ),
+    )
     einsum_form = "kba,kc->abc"
     hidden_total = hid_local * ch_count
     stat_sums = together((jnp.sum(triangle, 0), jnp.sum(triangle * triangle, 0)), "ch")

time: 322 us -> 537 us (1.67); the launches traced: 321 us -> 530 us
  waiting for transfers between devices: 212 us -> 423 us
  between operations: 14.3 us -> 1.18 us
  starting transfers between devices: 24.6 us -> 32.1 us
  local copies, waits for them, and re-layouts: 10.5 us -> 16.6 us
    all_to_all x0 -> x1, waiting for transfers between devices: none -> 414 us  [local(): lax.all_to_all(jnp.stack([left_side] * lax.axis_size(ROW)), ROW, 0, 0)]
    all_gather x1 -> x0, waiting for transfers between devices: 200 us -> none  [local(): lax.all_gather(left_side, ROW, axis=1, tiled=True)]
    all_to_all x0 -> x1, starting transfers between devices: none -> 7.67 us  [local(): lax.all_to_all(jnp.stack([left_side] * lax.axis_size(ROW)), ROW, 0, 0)]
    another operation x0 -> x1, local copies, waits for them, and re-layouts: none -> 7.19 us  [local(): jnp.stack([left_side] * lax.axis_size(ROW))]
  transfers between devices with their start and end apart: 4 -> 4, of which waited for: 4 -> 4; matrix products, arithmetic and copies ran while one was open for 4% -> 3% of each run, Pallas kernels for 0% -> 0%
where the time goes in v1:
time: 537 us; the launch traced here: 530 us
  waiting for transfers between devices  423 us (79%)
  matrix products  34.3 us (6%)
  starting transfers between devices  32.1 us (6%)
  local copies, waits for them, and re-layouts  16.6 us (3%)
  blocking collectives  15.6 us (3%)
  other arithmetic  7.43 us (1%)
    all_to_all x1, waiting for transfers between devices, local(): lax.all_to_all(jnp.stack([left_side] * lax.axis_size(ROW)), ROW, 0, 0)  414 us
    dot_general x1, matrix products, batched_rows(): lax.dot_general(first, second, (((2,), (2,)), ((0,), (0,))), preferred_el...  29.3 us
    all_to_all x1, starting transfers between devices, moved_by_axis(): whole = lax.all_to_all(whole, axes[k], k, k, tiled=True)  12.7 us
    psum x1, blocking collectives, packed_total(): so_far = lax.psum(vector, axis)  11.6 us
  transfers between devices with their start and end apart: 4, of which 4 were waited for; matrix products, arithmetic and copies ran while one was open for 3% of the time, Pallas kernels for 0%

profile of v1, /device:TPU:16, one launch (start us, length us, event | category | flops | bytes accessed | tf_op | source)
XLA Modules:
  0.0 530.3 jit_solution(11181164168743135752)
XLA Ops:
  0.6 1.3 reshape.156
  2.1 4.0 all_to_all.26
  6.0 1.0 copy.88
  7.0 12.7 %all-to-all-start.1 = ((bf16[64,2,3,3,128]{4,1,3,2,0:T(2,128)(2,1)}), bf16[64,2,3,3,128]{4,1,3,2,0:T(2,128)(2,1)S(1)}, u32[]{:S(2)}, u32[]{:S(2)}) async-start(bf16[64,2,3,3,128]{4,1,3,2,0:T(2,128)(2,1)} %copy.88), calls=%async_computation.1 | async-start | bytes 589824 | tf_op jit(solution)/shard_map/all_to_all | solution.py:27
  19.7 1.1 convert_reduce_fusion
  21.5 1.4 fusion.22
  23.1 1.5 fusion.6
  24.6 1.5 fusion.18
  26.1 7.7 %all-to-all-done.1 = bf16[64,2,3,3,128]{4,1,3,2,0:T(2,128)(2,1)S(1)} async-done(((bf16[64,2,3,3,128]{4,1,3,2,0:T(2,128)(2,1)}), bf16[64,2,3,3,128]{4,1,3,2,0:T(2,128)(2,1)S(1)}, u32[]{:S(2)}, u32[]{:S(2)}) %all-to-all-start.1) | async-done | bytes 294944 | tf_op jit(solution)/shard_map/all_to_all | solution.py:27
  33.8 7.2 %stack.2 = bf16[128,64,3,384]{3,1,2,0:T(8,128)(2,1)} broadcast(bf16[64,3,384]{2,0,1:T(8,128)(2,1)S(1)} %fusion.18), dimensions={1,2,3} | broadcast | bytes 19021824 | tf_op jit(solution)/shard_map/stack | solution.py:121
  41.0 7.7 %all-to-all-start.2 = ((bf16[128,64,3,384]{3,1,2,0:T(8,128)(2,1)}), bf16[128,64,3,384]{3,1,2,0:T(8,128)(2,1)}, u32[]{:S(2)}, u32[]{:S(2)}) async-start(bf16[128,64,3,384]{3,1,2,0:T(8,128)(2,1)} %stack.2), calls=%async_computation.2 | async-start | bytes 37748736 | tf_op jit(solution)/shard_map/all_to_all | solution.py:121
  50.4 0.9 convert_reduce_fusion.1
  51.4 2.0 fusion.26
  53.4 413.8 %all-to-all-done.2 = bf16[128,64,3,384]{3,1,2,0:T(8,128)(2,1)} async-done(((bf16[128,64,3,384]{3,1,2,0:T(8,128)(2,1)}), bf16[128,64,3,384]{3,1,2,0:T(8,128)(2,1)}, u32[]{:S(2)}, u32[]{:S(2)}) %all-to-all-start.2) | async-done | bytes 18874400 | tf_op jit(solution)/shard_map/all_to_all | solution.py:121
  467.2 29.3 %fusion.50 = (f32[3,384]{1,0:T(4,128)S(1)}, f32[3,384]{1,0:T(4,128)S(1)}, f32[64,3,384]{2,1,0:T(4,128)S(1)}) fusion(bf16[64,384,384]{2,0,1:T(8,128)(2,1)} %bitcast.11, bf16[64,3,384]{2,0,1:T(8,128)(2,1)S(1)} %fusion.19), kind=kOutput, calls=%fused_computation.78 | convolution fusion | flops 56841984 | bytes 19325952 | tf_op jit(solution)/shard_map/dot_general | solution.py:85
  496.6 0.8 broadcast_in_dim.2
  497.4 4.8 all-to-all-start.3
  502.3 1.3 copy.92
  504.6 0.7 copy.128
  505.3 7.0 %all-to-all-start.4 = ((bf16[2,384,3,64]{1,3,2,0:T(8,128)(2,1)}), bf16[2,384,3,64]{1,3,2,0:T(8,128)(2,1)S(1)}, u32[]{:S(2)}, u32[]{:S(2)}) async-start(bf16[2,384,3,64]{1,3,2,0:T(8,128)(2,1)} %bitcast.42), calls=%async_computation.4 | async-start | bytes 589824 | tf_op jit(solution)/shard_map/all_to_all | solution.py:57
  512.4 1.3 copy.95
  514.2 1.4 all-to-all-done.4
  517.0 11.6 %psum.7 = f32[2304]{0:T(1024)S(1)} all-reduce(f32[2304]{0:T(1024)S(1)} %pad_maximum_fusion.1), channel_id=1, replica_groups=mesh['row_0'=8,'row_1'=2,'row_2'=4,'row_3'=2,'ch'=2] {'ch'}, use_global_device_ids=true, to_apply=%region_10.0 | all-reduce | flops 2304 | bytes 18432 | tf_op jit(solution)/shard_map/psum | solution.py:63
  529.3 0.8 fusion.30
  (60 shorter events, 6.4 us)
Async XLA Ops:
  0.6 503.6 %copy-start = (bf16[128,128]{1,0:T(8,128)(2,1)S(1)}, bf16[128,128]{1,0:T(8,128)(2,1)}, u32[]{:S(2)}) copy-start(bf16[128,128]{1,0:T(8,128)(2,1)} %param.20) | copy-start | bytes 98308
  7.0 26.8 %all-to-all-start.1 = ((bf16[64,2,3,3,128]{4,1,3,2,0:T(2,128)(2,1)}), bf16[64,2,3,3,128]{4,1,3,2,0:T(2,128)(2,1)S(1)}, u32[]{:S(2)}, u32[]{:S(2)}) async-start(bf16[64,2,3,3,128]{4,1,3,2,0:T(2,128)(2,1)} %copy.88), calls=%async_computation.1 | async-start | bytes 589824 | tf_op jit(solution)/shard_map/all_to_all | solution.py:27
  41.0 7.7 %copy-start.6 = (f32[128]{0:T(128)S(1)}, f32[128]{0:T(128)}, u32[]{:S(2)}) copy-start(f32[128]{0:T(128)} %param.19) | copy-start | bytes 1540
  41.0 7.8 %copy-start.7 = (f32[128]{0:T(128)S(1)}, f32[128]{0:T(128)}, u32[]{:S(2)}) copy-start(f32[128]{0:T(128)} %param.21) | copy-start | bytes 1540
  41.0 7.9 %copy-start.1 = (bf16[3,384,128]{2,1,0:T(8,128)(2,1)S(1)}, bf16[3,384,128]{2,1,0:T(8,128)(2,1)}, u32[]{:S(2)}) copy-start(bf16[3,384,128]{2,1,0:T(8,128)(2,1)} %param.11) | copy-start | bytes 884740
  41.0 7.9 %copy-start.4 = (bf16[128,64]{0,1:T(8,128)(2,1)S(1)}, bf16[128,64]{0,1:T(8,128)(2,1)}, u32[]{:S(2)}) copy-start(bf16[128,64]{0,1:T(8,128)(2,1)} %param.17) | copy-start | bytes 49156
  41.0 7.9 %copy-start.8 = (f32[128]{0:T(128)S(1)}, f32[128]{0:T(128)}, u32[]{:S(2)}) copy-start(f32[128]{0:T(128)} %param.13) | copy-start | bytes 1540
  41.0 8.4 %copy-start.5 = (bf16[128,64]{0,1:T(8,128)(2,1)S(1)}, bf16[128,64]{0,1:T(8,128)(2,1)}, u32[]{:S(2)}) copy-start(bf16[128,64]{0,1:T(8,128)(2,1)} %param.16) | copy-start | bytes 49156
  41.0 426.1 %all-to-all-start.2 = ((bf16[128,64,3,384]{3,1,2,0:T(8,128)(2,1)}), bf16[128,64,3,384]{3,1,2,0:T(8,128)(2,1)}, u32[]{:S(2)}, u32[]{:S(2)}) async-start(bf16[128,64,3,384]{3,1,2,0:T(8,128)(2,1)} %stack.2), calls=%async_computation.2 | async-start | bytes 37748736 | tf_op jit(solution)/shard_map/all_to_all | solution.py:121
  48.7 466.9 %copy-start.3 = (bf16[128,128]{1,0:T(8,128)(2,1)S(1)}, bf16[128,128]{1,0:T(8,128)(2,1)}, u32[]{:S(2)}) copy-start(bf16[128,128]{1,0:T(8,128)(2,1)} %param.18) | copy-start | bytes 98308
  497.4 6.6 %all-to-all-start.3 = ((f32[2,1,2304]{2,1,0:T(1,128)}), f32[2,1,2304]{2,1,0:T(1,128)S(1)}, u32[]{:S(2)}, u32[]{:S(2)}) async-start(f32[2,1,2304]{2,1,0:T(1,128)} %broadcast_in_dim.2), calls=%async_computation.3 | async-start | bytes 36864 | tf_op jit(solution)/shard_map/all_to_all | solution.py:39
  505.3 10.3 %all-to-all-start.4 = ((bf16[2,384,3,64]{1,3,2,0:T(8,128)(2,1)}), bf16[2,384,3,64]{1,3,2,0:T(8,128)(2,1)S(1)}, u32[]{:S(2)}, u32[]{:S(2)}) async-start(bf16[2,384,3,64]{1,3,2,0:T(8,128)(2,1)} %bitcast.42), calls=%async_computation.4 | async-start | bytes 589824 | tf_op jit(solution)/shard_map/all_to_all | solution.py:57
  516.3 13.8 %copy-start.2 = (bf16[384,3,64]{0,2,1:T(8,128)(2,1)}, bf16[384,3,64]{0,2,1:T(8,128)(2,1)S(1)}, u32[]{:S(2)}) copy-start(bf16[384,3,64]{0,2,1:T(8,128)(2,1)S(1)} %get-tuple-element.11) | copy-start | bytes 442372
